TPU v7x, 32 devices: a whole 2x2x4 slice. The times are simulated.
32 devices in a mesh: users: 8 (over z, x), items: 4 (over y, core).
Axes of the slice: x: 2, y: 2, z: 4, core: 2. Of those that a mesh axis runs over, the one named last changes fastest.
Arguments:
- tile_users: int32 [8, 4, 128], P('users', 'items'), may hold values from 0 to 127
- tile_owners: int32 [8, 4, 128, 1], P('users', 'items'), may hold values from 0 to 7; in each aligned block of 128 rows (0 to 127, 128 to 255, ..., all dimensions but the last counted through in order) at most 32 rows name the same one
- tile_blocks: int32 [8, 4, 128], P('users', 'items'), may hold values from 0 to 63
- tile_contexts: int32 [8, 4, 128], P('users', 'items'), may hold values from 0 to 7
- row_users: int32 [8, 4, 128, 128], P('users', 'items'), may hold values from 0 to 15
- row_items: int32 [8, 4, 128, 128], P('users', 'items'), may hold values from 0 to 15
- row_contexts: int32 [8, 4, 128, 128], P('users', 'items'), may hold values from 0 to 127
- tile_values: bfloat16 [8, 4, 128, 128], P('users', 'items'), may hold values from -49152 to 49152
- tile_count: int32 [8, 4], P('users', 'items'), may hold values from 64 to 128, as said below
- item_factors: bfloat16 [8192, 256], P('users'), may hold values from -0.125 to 0.25
- context_factors: bfloat16 [1024, 256], replicated, may hold values from -0.125 to 0.25
- profile: bfloat16 [16384, 2048], P('users', 'items'), may hold values from -192 to 192
- feature_factors: bfloat16 [2048, 256], P('items'), may hold values from -6 to 6
Outputs:
- user_factors: bfloat16 [16384, 256], P('users')
- feature_new: bfloat16 [2048, 256], P('items')
Inputs may be any that keep to these rules, and one draw needn't show every extreme that they name: On one device at most 32 tiles name one index of users in tile_owners, a bound that some block reaches. The live tiles of a device are its first tile_count tiles; some device has all 128 live.
All inputs are finite; a program needn't handle non-finite values.
Results may differ from a plain program's by a relative error of at most 0.00155.
The roundings to bfloat16 on the way count: a program that leaves them out, or rounds other values in their place, can miss the bound.
Values may be sent and summed in bfloat16 or wider, within the bound.
No kernel may reach another device: no remote copies, remote signals or barrier semaphores. Data moves between devices by JAX's collectives and lax.ppermute only.
A program may use at most 64 MiB of HBM per device.

v0:
```python
import jax
import jax.numpy as jnp
from jax import lax
from jax.sharding import PartitionSpec as P

CB = 128
IB = 16
UB = 16
RIDGE = 1.0


def gram(matrix):
    return lax.dot_general(
        matrix, matrix, (((0,), (0,)), ((), ())), preferred_element_type=jnp.float32
    )


def solve_rows(normal, right_side):
    cholesky_factor = jnp.linalg.cholesky(normal)
    return jax.scipy.linalg.cho_solve((cholesky_factor, True), right_side.T).T


def local(
    tile_users,
    tile_owners,
    tile_blocks,
    tile_contexts,
    row_users,
    row_items,
    row_contexts,
    tile_values,
    tile_count,
    item_factors,
    context_factors,
    profile,
    feature_factors,
):
    users_size = lax.axis_size("users")
    tile_total = tile_users.shape[2]
    rank_width = item_factors.shape[1]
    slab_users = profile.shape[0]
    blocks_held = item_factors.shape[0] // IB
    capacity = max(2, 2 * tile_total // users_size)
    owners = tile_owners.reshape(tile_total)
    local_block = tile_blocks.reshape(tile_total)
    live_count = tile_count.reshape(())
    position = jnp.arange(tile_total, dtype=jnp.int32)
    same_owner = (owners[:, None] == owners[None, :]) & (position[None, :] < position[:, None])
    slot_rank = jnp.sum(same_owner.astype(jnp.int32), axis=1)
    tile_place = owners * capacity + slot_rank
    request_block = jnp.where(position < live_count, local_block, 0)
    wanted = jnp.zeros((users_size * capacity,), jnp.int32).at[tile_place].set(request_block)
    asked_blocks = lax.all_to_all(
        wanted.reshape(users_size, capacity), "users", split_axis=0, concat_axis=0, tiled=True
    )
    shard_blocks = item_factors.reshape(blocks_held, IB, rank_width)
    answered = shard_blocks[asked_blocks.reshape(-1)].reshape(users_size, capacity, IB, rank_width)
    fetched = lax.all_to_all(answered, "users", split_axis=0, concat_axis=0, tiled=True).reshape(
        users_size * capacity, IB, rank_width
    )
    identity = jnp.eye(rank_width, dtype=jnp.float32)
    context_gram = gram(context_factors)
    item_gram = lax.psum(gram(item_factors), "users")
    feature_gram = lax.psum(gram(feature_factors), "items")
    normal = item_gram * context_gram + feature_gram
    normal = normal + RIDGE * identity
    user_blocks = slab_users // UB
    context_table = context_factors.reshape(-1, CB, rank_width)
    tile_ublock = tile_users.reshape(tile_total)
    tile_cblock = tile_contexts.reshape(tile_total)
    users_rows = row_users.reshape(tile_total, -1)
    items_rows = row_items.reshape(tile_total, -1)
    contexts_rows = row_contexts.reshape(tile_total, -1)
    values_rows = tile_values.reshape(tile_total, -1)
    group_size = 16

    def add_group(step_index, running):
        first_tile = step_index * group_size

        def window(source):
            return lax.dynamic_slice_in_dim(source, first_tile, group_size, 0)

        item_blocks = fetched[window(tile_place)]
        context_blocks = context_table[window(tile_cblock)]
        item_onehot = (
            window(items_rows)[:, :, None] == jnp.arange(IB, dtype=jnp.int32)[None, None, :]
        ).astype(jnp.bfloat16)
        context_onehot = (
            window(contexts_rows)[:, :, None] == jnp.arange(CB, dtype=jnp.int32)[None, None, :]
        ).astype(jnp.bfloat16)
        item_rows_sel = jnp.einsum(
            "gti,gir->gtr", item_onehot, item_blocks, preferred_element_type=jnp.float32
        )
        context_rows_sel = jnp.einsum(
            "gtc,gcr->gtr", context_onehot, context_blocks, preferred_element_type=jnp.float32
        )
        alive_mask = (first_tile + jnp.arange(group_size, dtype=jnp.int32) < live_count).astype(
            jnp.float32
        )
        weighted = window(values_rows).astype(jnp.float32) * alive_mask[:, None]
        row_terms = weighted[:, :, None] * item_rows_sel * context_rows_sel
        user_onehot = (
            window(users_rows)[:, None, :] == jnp.arange(UB, dtype=jnp.int32)[None, :, None]
        ).astype(jnp.float32)
        per_tile = jnp.einsum(
            "gut,gtr->gur", user_onehot, row_terms, precision=lax.Precision.HIGHEST
        )
        block_onehot = (
            window(tile_ublock)[None, :] == jnp.arange(user_blocks, dtype=jnp.int32)[:, None]
        ).astype(jnp.float32)
        return running + jnp.einsum(
            "bg,gur->bur", block_onehot, per_tile, precision=lax.Precision.HIGHEST
        )

    rounds = (live_count + group_size - 1) // group_size
    mttkrp = lax.fori_loop(
        0, rounds, add_group, jnp.zeros((user_blocks, UB, rank_width), jnp.float32)
    ).reshape(slab_users, rank_width)
    local_right = mttkrp + jnp.dot(profile, feature_factors, preferred_element_type=jnp.float32)
    right_side = lax.psum(local_right, "items")
    user_factors = solve_rows(normal, right_side).astype(jnp.bfloat16)
    feature_terms = lax.dot_general(
        profile, user_factors, (((0,), (0,)), ((), ())), preferred_element_type=jnp.float32
    )
    user_gram, feature_right = lax.psum((gram(user_factors), feature_terms), "users")
    feature_new = solve_rows(user_gram + RIDGE * identity, feature_right).astype(jnp.bfloat16)
    return (user_factors, feature_new)


def solution(mesh):
    in_specs = (
        P("users", "items", None),
        P("users", "items", None, None),
        P("users", "items", None),
        P("users", "items", None),
        P("users", "items", None, None),
        P("users", "items", None, None),
        P("users", "items", None, None),
        P("users", "items", None, None),
        P("users", "items"),
        P("users", None),
        P(),
        P("users", "items"),
        P("items", None),
    )
    out_specs = (P("users", None), P("items", None))
    return jax.shard_map(local, mesh=mesh, in_specs=in_specs, out_specs=out_specs, check_vma=False)
```

profile of v0, /device:TPU:0, one launch (start us, length us, event | category | flops | bytes accessed | tf_op | source)
XLA Modules:
  0.0 481.4 jit_solution(13912460111386983107)
XLA Ops:
  11.3 13.6 %all_to_all.14 = s32[8,1,32]{2,1,0:T(1,128)S(1)} all-to-all(s32[8,1,32]{2,1,0:T(1,128)S(1)} %all_to_all.9), channel_id=1, replica_groups=mesh['users'=8,'items'=4] {'users'}, dimensions={0} | all-to-all | bytes 2048 | tf_op jit(solution)/shard_map/all_to_all | solution.py:53
  29.2 4.5 all-to-all-start.1
  35.9 48.9 %all-to-all-done.1 = bf16[8,32,16,256]{3,2,1,0:T(8,128)(2,1)} async-done(((bf16[8,32,16,256]{3,2,1,0:T(8,128)(2,1)}), bf16[8,32,16,256]{3,2,1,0:T(8,128)(2,1)}, u32[]{:S(2)}, u32[]{:S(2)}) %all-to-all-start.1) | async-done | bytes 2097184 | tf_op jit(solution)/shard_map/all_to_all | solution.py:58
  86.4 115.0 %while.12 = (s32[]{:T(128)}, f32[128,16,256]{2,0,1:T(8,128)}, s32[]{:T(128)}, s32[128]{0:T(128)S(1)}, s32[128,128]{1,0:T(8,128)}, /*index=5*/bf16[128,128]{1,0:T...) while((s32[]{:T(128)}, f32[128,16,256]{2,0,1:T(8,128)}, ...), condition=%wide.region_9.11_spmd, body=%wide.region_8.10_spmd.sunk | while | flops 354230400 | bytes 25138244 | solution.py:116
  96.7 4.0 convolution_add_fusion.3
  111.1 4.0 convolution_add_fusion.3
  125.5 4.0 convolution_add_fusion.3
  139.9 4.0 convolution_add_fusion.3
  154.3 4.0 convolution_add_fusion.3
  168.6 4.0 convolution_add_fusion.3
  183.0 4.0 convolution_add_fusion.3
  197.4 4.0 convolution_add_fusion.3
  206.9 54.0 %all-reduce.11.cloned.1.call-done = (f32[256,2048]{0,1:T(8,128)}, f32[256,256]{0,1:T(8,128)}) async-done(((f32[256,2048]{0,1:T(8,128)}, f32[256,256]{0,1:T(8,128)}), (f32[256,2048]{0,1:T(8,128)}, f32[256,256]{0,1:T(8,128)})) %all-reduce.11.cloned.1.call-update) | async-done | bytes 2359312 | tf_op jit(solution)/shard_map/psum | solution.py:120
  262.5 11.7 %cholesky.130 = f32[128,128]{1,0:T(8,128)S(1)} custom-call(f32[128,128]{1,0:T(8,128)S(1)} %cholesky.194), custom_call_target="Cholesky" | custom-call | tf_op jit(solution)/shard_map/jit(cholesky)/cholesky | solution.py:19
  274.3 9.8 %custom-call.25 = f32[1,128,128]{1,2,0:T(8,128)S(1)} custom-call(f32[1,128,128]{2,1,0:T(8,128)S(1)} %get-tuple-element.153), custom_call_target="InvertDiagBlocksLowerTriangular" | custom-call | tf_op jit(solution)/shard_map/jit(cholesky)/cholesky | solution.py:19
  284.6 11.7 %cholesky.147 = f32[128,128]{1,0:T(8,128)S(1)} custom-call(f32[128,128]{1,0:T(8,128)S(1)} %convolution_subtract_fusion.5), custom_call_target="Cholesky" | custom-call | tf_op jit(solution)/shard_map/jit(cholesky)/cholesky | solution.py:19
  298.4 4.2 while.13
  302.6 19.7 %custom-call.22 = f32[2,128,128]{1,2,0:T(8,128)S(1)} custom-call(f32[2,128,128]{2,1,0:T(8,128)S(1)} %get-tuple-element.79), custom_call_target="InvertDiagBlocksLowerTriangular" | custom-call | tf_op jit(solution)/shard_map/jit(_cho_solve)/triangular_solve | solution.py:20
  336.2 72.6 %all-reduce.9.cloned.1.call-done = (f32[256,512]{1,0:T(8,128)}, f32[256,256]{0,1:T(8,128)}) async-done(((f32[256,512]{1,0:T(8,128)}, f32[256,256]{0,1:T(8,128)}), (f32[256,512]{1,0:T(8,128)}, f32[256,256]{0,1:T(8,128)})) %all-reduce.9.cloned.1.call-update) | async-done | bytes 786448 | tf_op jit(solution)/shard_map/psum | solution.py:125
  411.0 11.7 %cholesky.164 = f32[128,128]{1,0:T(8,128)S(1)} custom-call(f32[128,128]{1,0:T(8,128)S(1)} %cholesky.197), custom_call_target="Cholesky" | custom-call | tf_op jit(solution)/shard_map/jit(cholesky)/cholesky | solution.py:19
  422.8 9.8 %custom-call.26 = f32[1,128,128]{1,2,0:T(8,128)S(1)} custom-call(f32[1,128,128]{2,1,0:T(8,128)S(1)} %get-tuple-element.149), custom_call_target="InvertDiagBlocksLowerTriangular" | custom-call | tf_op jit(solution)/shard_map/jit(cholesky)/cholesky | solution.py:19
  433.1 11.7 %cholesky.181 = f32[128,128]{1,0:T(8,128)S(1)} custom-call(f32[128,128]{1,0:T(8,128)S(1)} %convolution_subtract_fusion.4), custom_call_target="Cholesky" | custom-call | tf_op jit(solution)/shard_map/jit(cholesky)/cholesky | solution.py:19
  447.5 3.9 while.14
  451.4 19.9 %custom-call.23 = f32[2,128,128]{1,2,0:T(8,128)S(1)} custom-call(f32[2,128,128]{2,1,0:T(8,128)S(1)} %get-tuple-element.87), custom_call_target="InvertDiagBlocksLowerTriangular" | custom-call | tf_op jit(solution)/shard_map/jit(_cho_solve)/triangular_solve | solution.py:20
  (223 shorter events, 131.3 us)
Async XLA Ops:
  7.2 197.0 %copy-start = (bf16[2048,512]{1,0:T(8,128)(2,1)S(1)}, bf16[2048,512]{1,0:T(8,128)(2,1)}, u32[]{:S(2)}) copy-start(bf16[2048,512]{1,0:T(8,128)(2,1)} %param.27) | copy-start | bytes 6291460
  29.2 4.6 copy-start.3
  29.2 5.7 %copy-start.10 = (s32[1,1,128,1]{2,3,1,0:T(1,128)S(1)}, s32[1,1,128,1]{2,3,1,0:T(1,128)}, u32[]{:S(2)}) copy-start(s32[1,1,128,1]{2,3,1,0:T(1,128)} %param.17) | copy-start | bytes 1540
  29.2 5.7 %copy-start.4 = (bf16[512,256]{1,0:T(8,128)(2,1)S(1)}, bf16[512,256]{1,0:T(8,128)(2,1)}, u32[]{:S(2)}) copy-start(bf16[512,256]{1,0:T(8,128)(2,1)} %param.28) | copy-start | bytes 786436
  29.2 55.6 %all-to-all-start.1 = ((bf16[8,32,16,256]{3,2,1,0:T(8,128)(2,1)}), bf16[8,32,16,256]{3,2,1,0:T(8,128)(2,1)}, u32[]{:S(2)}, u32[]{:S(2)}) async-start(bf16[8,32,16,256]{3,2,1,0:T(8,128)(2,1)} %bitcast.133), calls=%async_computation.1 | async-start | bytes 4194304 | tf_op jit(solution)/shard_map/all_to_all | solution.py:58
  33.7 52.7 %copy-start.9 = (s32[1,1,128]{2,1,0:T(1,128)S(1)}, s32[1,1,128]{2,1,0:T(1,128)}, u32[]{:S(2)}) copy-start(s32[1,1,128]{2,1,0:T(1,128)} %param.19) | copy-start | bytes 1540
  33.7 52.7 %copy-start.11 = (s32[1,1,128]{2,1,0:T(1,128)S(1)}, s32[1,1,128]{2,1,0:T(1,128)}, u32[]{:S(2)}) copy-start(s32[1,1,128]{2,1,0:T(1,128)} %param.16) | copy-start | bytes 1540
  33.7 173.2 %all-reduce.7.cloned.1.call-start = ((), (), s32[]{:S(2)}) async-start(), calls=%async_computation.2 | async-start | bytes 524288 | tf_op jit(solution)/shard_map/psum | solution.py:63
  34.8 226.1 %all-reduce.11.cloned.1.call-start = ((), (), s32[]{:S(2)}) async-start(), calls=%async_computation.4 | async-start | bytes 4718592 | tf_op jit(solution)/shard_map/psum | solution.py:120
  92.8 2.9 copy-start.1
  107.2 2.9 copy-start.1
  121.6 2.9 copy-start.1
  136.0 2.9 copy-start.1
  150.3 2.9 copy-start.1
  164.7 2.9 copy-start.1
  179.1 2.9 copy-start.1
  193.4 2.9 copy-start.1
  206.2 54.7 %copy-start.2 = (bf16[8,128,256]{2,1,0:T(8,128)(2,1)S(1)}, bf16[8,128,256]{2,1,0:T(8,128)(2,1)}, u32[]{:S(2)}) copy-start(bf16[8,128,256]{2,1,0:T(8,128)(2,1)} %get-tuple-element.400) | copy-start | bytes 1572868
  206.3 202.6 %all-reduce.9.cloned.1.call-start = ((), (), s32[]{:S(2)}) async-start(), calls=%async_computation.3 | async-start | bytes 1572864 | tf_op jit(solution)/shard_map/psum | solution.py:125
  322.2 2.5 copy-start.5
  328.6 3.3 copy-start.7
  330.7 1.2 copy-start.6
  409.8 61.5 %copy-start.8 = (f32[256,512]{1,0:T(8,128)S(1)}, f32[256,512]{1,0:T(8,128)}, u32[]{:S(2)}) copy-start(f32[256,512]{1,0:T(8,128)} %get-tuple-element.134) | copy-start | bytes 1572868
Sparse Core Ops, SparseCore 0:
  38.5 86.4 all-reduce.6
  206.4 54.4 all-reduce.10
  333.6 75.2 all-reduce.8
where the time goes:
time: 489 us; the launch traced here: 481 us
  waiting for transfers between devices  176 us (36%)
  other arithmetic  126 us (26%)
  matrix products  80.1 us (16%)
  local copies, waits for them, and re-layouts  62.1 us (13%)
  between operations  17.8 us (4%)
  blocking collectives  13.6 us (3%)
  starting transfers between devices  5.11 us (1%)
    psum x1, waiting for transfers between devices, local(): lax.psum((gram(user_factors), feature_terms), 'users')  72.6 us
    another operation x13, other arithmetic, solve_rows(): cholesky_factor = jnp.linalg.cholesky(normal)  68.6 us
    psum x1, waiting for transfers between devices, local(): right_side = lax.psum(local_right, 'items')  54 us
    all_to_all x1, waiting for transfers between devices, local(): lax.all_to_all(answered, 'users', split_axis=0, concat_axis=0, tiled=True)  48.9 us
    another operation x5, other arithmetic, solve_rows(): return jax.scipy.linalg.cho_solve((cholesky_factor, True), right_side.T).T  39.7 us
    dot_general x8, matrix products, add_group(): jnp.einsum('bg,gur->bur', block_onehot, per_tile, precision=lax.Precision...  32 us
    gather x8, local copies, waits for them, and re-layouts, add_group(): item_blocks = fetched[window(tile_place)]  17.2 us
    dot_general x8, matrix products, add_group(): jnp.einsum('gtc,gcr->gtr', context_onehot, context_blocks, preferred_elem...  14.5 us
  transfers between devices with their start and end apart: 4, of which 3 were waited for; matrix products, arithmetic and copies ran while one was open for 26% of the time, Pallas kernels for 0%

commit v1 on v0

--- a/solution.py
+++ b/solution.py
@@ -117,7 +117,7 @@
         0, rounds, add_group, jnp.zeros((user_blocks, UB, rank_width), jnp.float32)
     ).reshape(slab_users, rank_width)
     local_right = mttkrp + jnp.dot(profile, feature_factors, preferred_element_type=jnp.float32)
-    right_side = lax.psum(local_right, "items")
+    right_side = jnp.sum(lax.all_gather(local_right, "items"), axis=0)
     user_factors = solve_rows(normal, right_side).astype(jnp.bfloat16)
     feature_terms = lax.dot_general(
         profile, user_factors, (((0,), (0,)), ((), ())), preferred_element_type=jnp.float32

time: 489 us -> 436 us (0.89)
  waiting for transfers between devices: 176 us -> 117 us
  other arithmetic: 126 us -> 132 us
    psum x1, waiting for transfers between devices: 54 us -> 0.02 us  [local(): feature_gram = lax.psum(gram(feature_factors), 'items')]
    reduce_sum x0 -> x1, other arithmetic: none -> 5.6 us  [local(): right_side = jnp.sum(lax.all_gather(local_right, 'items'), axis=0)]
  transfers between devices with their start and end apart: 4 -> 5, of which waited for: 3 -> 2; matrix products, arithmetic and copies ran while one was open for 26% -> 43% of each run, Pallas kernels for 0% -> 0%
where the time goes in v1:
time: 436 us; the launch traced here: 428 us
  other arithmetic  132 us (30%)
  waiting for transfers between devices  117 us (27%)
  matrix products  80.2 us (18%)
  local copies, waits for them, and re-layouts  62.4 us (14%)
  between operations  17.8 us (4%)
  blocking collectives  13.6 us (3%)
  starting transfers between devices  5.16 us (1%)
    psum x1, waiting for transfers between devices, local(): lax.psum((gram(user_factors), feature_terms), 'users')  71.7 us
    another operation x13, other arithmetic, solve_rows(): cholesky_factor = jnp.linalg.cholesky(normal)  68.5 us
    all_to_all x1, waiting for transfers between devices, local(): lax.all_to_all(answered, 'users', split_axis=0, concat_axis=0, tiled=True)  44.8 us
    another operation x5, other arithmetic, solve_rows(): return jax.scipy.linalg.cho_solve((cholesky_factor, True), right_side.T).T  39.7 us
    dot_general x8, matrix products, add_group(): jnp.einsum('bg,gur->bur', block_onehot, per_tile, precision=lax.Precision...  32 us
    gather x8, local copies, waits for them, and re-layouts, add_group(): item_blocks = fetched[window(tile_place)]  17.2 us
    dot_general x8, matrix products, add_group(): jnp.einsum('gtc,gcr->gtr', context_onehot, context_blocks, preferred_elem...  14.5 us
    all_to_all x1, blocking collectives, local(): lax.all_to_all(wanted.reshape(users_size, capacity), 'users', split_axis=...  13.6 us
  transfers between devices with their start and end apart: 5, of which 2 were waited for; matrix products, arithmetic and copies ran while one was open for 43% of the time, Pallas kernels for 0%

profile of v1, /device:TPU:0, one launch (start us, length us, event | category | flops | bytes accessed | tf_op | source)
XLA Modules:
  0.0 428.5 jit_solution(12400405044412644359)
XLA Ops:
  11.3 13.6 %all_to_all.14 = s32[8,1,32]{2,1,0:T(1,128)S(1)} all-to-all(s32[8,1,32]{2,1,0:T(1,128)S(1)} %all_to_all.9), channel_id=1, replica_groups=mesh['users'=8,'items'=4] {'users'}, dimensions={0} | all-to-all | bytes 2048 | tf_op jit(solution)/shard_map/all_to_all | solution.py:53
  29.2 4.5 %all-to-all-start.1 = ((bf16[8,32,16,256]{3,2,1,0:T(8,128)(2,1)}), bf16[8,32,16,256]{3,2,1,0:T(8,128)(2,1)}, u32[]{:S(2)}, u32[]{:S(2)}) async-start(bf16[8,32,16,256]{3,2,1,0:T(8,128)(2,1)} %bitcast.133), calls=%async_computation.1 | async-start | bytes 4194304 | tf_op jit(solution)/shard_map/all_to_all | solution.py:58
  36.0 44.8 %all-to-all-done.1 = bf16[8,32,16,256]{3,2,1,0:T(8,128)(2,1)} async-done(((bf16[8,32,16,256]{3,2,1,0:T(8,128)(2,1)}), bf16[8,32,16,256]{3,2,1,0:T(8,128)(2,1)}, u32[]{:S(2)}, u32[]{:S(2)}) %all-to-all-start.1) | async-done | bytes 2097184 | tf_op jit(solution)/shard_map/all_to_all | solution.py:58
  82.3 115.1 %while.12 = (s32[]{:T(128)}, f32[128,16,256]{2,0,1:T(8,128)}, s32[]{:T(128)}, s32[128]{0:T(128)S(1)}, s32[128,128]{1,0:T(8,128)}, /*index=5*/bf16[128,128]{1,0:T...) while((s32[]{:T(128)}, f32[128,16,256]{2,0,1:T(8,128)}, ...), condition=%wide.region_9.11_spmd, body=%wide.region_8.10_spmd.sunk | while | flops 354230400 | bytes 25138244 | solution.py:116
  92.7 4.0 convolution_add_fusion.3
  107.1 4.0 convolution_add_fusion.3
  121.5 4.0 convolution_add_fusion.3
  135.9 4.0 convolution_add_fusion.3
  150.3 4.0 convolution_add_fusion.3
  164.6 4.0 convolution_add_fusion.3
  179.0 4.0 convolution_add_fusion.3
  193.4 4.0 convolution_add_fusion.3
  204.9 11.7 %cholesky.130 = f32[128,128]{1,0:T(8,128)S(1)} custom-call(f32[128,128]{1,0:T(8,128)S(1)} %cholesky.194), custom_call_target="Cholesky" | custom-call | tf_op jit(solution)/shard_map/jit(cholesky)/cholesky | solution.py:19
  216.7 9.8 %custom-call.25 = f32[1,128,128]{1,2,0:T(8,128)S(1)} custom-call(f32[1,128,128]{2,1,0:T(8,128)S(1)} %get-tuple-element.151), custom_call_target="InvertDiagBlocksLowerTriangular" | custom-call | tf_op jit(solution)/shard_map/jit(cholesky)/cholesky | solution.py:19
  227.0 11.7 %cholesky.147 = f32[128,128]{1,0:T(8,128)S(1)} custom-call(f32[128,128]{1,0:T(8,128)S(1)} %convolution_subtract_fusion.5), custom_call_target="Cholesky" | custom-call | tf_op jit(solution)/shard_map/jit(cholesky)/cholesky | solution.py:19
  240.8 4.2 while.13
  245.0 19.7 %custom-call.22 = f32[2,128,128]{1,2,0:T(8,128)S(1)} custom-call(f32[2,128,128]{2,1,0:T(8,128)S(1)} %get-tuple-element.79), custom_call_target="InvertDiagBlocksLowerTriangular" | custom-call | tf_op jit(solution)/shard_map/jit(_cho_solve)/triangular_solve | solution.py:20
  264.7 5.6 %reduce_sum.22 = f32[2048,256]{1,0:T(8,128)} reduce(f32[4,2048,256]{2,1,0:T(8,128)} %bitcast.134, f32[]{:T(128)} %constant.121.clone.1), dimensions={0}, to_apply=%region_10.12 | reduce | flops 1572864 | bytes 10485764 | tf_op jit(solution)/shard_map/reduce_sum | solution.py:120
  284.4 71.7 %all-reduce.10.cloned.1.call-done = (f32[256,512]{1,0:T(8,128)}, f32[256,256]{0,1:T(8,128)}) async-done(((f32[256,512]{1,0:T(8,128)}, f32[256,256]{0,1:T(8,128)}), (f32[256,512]{1,0:T(8,128)}, f32[256,256]{0,1:T(8,128)})) %all-reduce.10.cloned.1.call-update) | async-done | bytes 786448 | tf_op jit(solution)/shard_map/psum | solution.py:125
  358.2 11.7 %cholesky.164 = f32[128,128]{1,0:T(8,128)S(1)} custom-call(f32[128,128]{1,0:T(8,128)S(1)} %cholesky.197), custom_call_target="Cholesky" | custom-call | tf_op jit(solution)/shard_map/jit(cholesky)/cholesky | solution.py:19
  370.0 9.8 %custom-call.26 = f32[1,128,128]{1,2,0:T(8,128)S(1)} custom-call(f32[1,128,128]{2,1,0:T(8,128)S(1)} %get-tuple-element.147), custom_call_target="InvertDiagBlocksLowerTriangular" | custom-call | tf_op jit(solution)/shard_map/jit(cholesky)/cholesky | solution.py:19
  380.3 11.7 %cholesky.181 = f32[128,128]{1,0:T(8,128)S(1)} custom-call(f32[128,128]{1,0:T(8,128)S(1)} %convolution_subtract_fusion.4), custom_call_target="Cholesky" | custom-call | tf_op jit(solution)/shard_map/jit(cholesky)/cholesky | solution.py:19
  394.6 3.8 while.14
  398.4 19.9 %custom-call.23 = f32[2,128,128]{1,2,0:T(8,128)S(1)} custom-call(f32[2,128,128]{2,1,0:T(8,128)S(1)} %get-tuple-element.87), custom_call_target="InvertDiagBlocksLowerTriangular" | custom-call | tf_op jit(solution)/shard_map/jit(_cho_solve)/triangular_solve | solution.py:20
  (227 shorter events, 131.9 us)
Async XLA Ops:
  7.2 193.0 %copy-start = (bf16[2048,512]{1,0:T(8,128)(2,1)S(1)}, bf16[2048,512]{1,0:T(8,128)(2,1)}, u32[]{:S(2)}) copy-start(bf16[2048,512]{1,0:T(8,128)(2,1)} %param.27) | copy-start | bytes 6291460
  29.2 4.5 %copy-start.5 = (bf16[512,256]{1,0:T(8,128)(2,1)S(1)}, bf16[512,256]{1,0:T(8,128)(2,1)}, u32[]{:S(2)}) copy-start(bf16[512,256]{1,0:T(8,128)(2,1)} %param.28) | copy-start | bytes 786436
  29.2 5.6 %copy-start.3 = (bf16[1024,256]{1,0:T(8,128)(2,1)S(1)}, bf16[1024,256]{1,0:T(8,128)(2,1)}, u32[]{:S(2)}) copy-start(bf16[1024,256]{1,0:T(8,128)(2,1)} %param.25) | copy-start | bytes 1572868
  29.2 51.6 %all-to-all-start.1 = ((bf16[8,32,16,256]{3,2,1,0:T(8,128)(2,1)}), bf16[8,32,16,256]{3,2,1,0:T(8,128)(2,1)}, u32[]{:S(2)}, u32[]{:S(2)}) async-start(bf16[8,32,16,256]{3,2,1,0:T(8,128)(2,1)} %bitcast.133), calls=%async_computation.1 | async-start | bytes 4194304 | tf_op jit(solution)/shard_map/all_to_all | solution.py:58
  33.7 2.3 copy-start.10
  33.7 169.3 %all-reduce.8.cloned.1.call-start = ((), (), s32[]{:S(2)}) async-start(), calls=%async_computation.3 | async-start | bytes 524288 | tf_op jit(solution)/shard_map/psum | solution.py:64
  34.7 47.6 %copy-start.9 = (s32[1,1,128]{2,1,0:T(1,128)S(1)}, s32[1,1,128]{2,1,0:T(1,128)}, u32[]{:S(2)}) copy-start(s32[1,1,128]{2,1,0:T(1,128)} %param.19) | copy-start | bytes 1540
  34.7 47.6 %copy-start.11 = (s32[1,1,128]{2,1,0:T(1,128)S(1)}, s32[1,1,128]{2,1,0:T(1,128)}, u32[]{:S(2)}) copy-start(s32[1,1,128]{2,1,0:T(1,128)} %param.16) | copy-start | bytes 1540
  34.8 168.2 %all-reduce.6.cloned.1.call-start = ((), (), s32[]{:S(2)}) async-start(), calls=%async_computation.2 | async-start | bytes 524288 | tf_op jit(solution)/shard_map/psum | solution.py:63
  35.9 228.8 %all-gather.3.cloned.1.call-start = ((), (), s32[]{:S(2)}) async-start(), calls=%async_computation.4 | async-start | bytes 10485760 | tf_op jit(solution)/shard_map/all_gather | solution.py:120
  88.8 2.9 copy-start.1
  103.1 2.9 copy-start.1
  117.5 2.9 copy-start.1
  131.9 2.9 copy-start.1
  146.3 2.9 copy-start.1
  160.7 2.9 copy-start.1
  175.1 2.9 copy-start.1
  189.4 2.9 copy-start.1
  202.3 1.0 copy-start.2
  202.4 153.7 %all-reduce.10.cloned.1.call-start = ((), (), s32[]{:S(2)}) async-start(), calls=%async_computation.5 | async-start | bytes 1572864 | tf_op jit(solution)/shard_map/psum | solution.py:125
  270.3 2.4 copy-start.4
  276.7 3.3 copy-start.7
  278.8 1.2 copy-start.6
  357.0 61.3 %copy-start.8 = (f32[256,512]{1,0:T(8,128)S(1)}, f32[256,512]{1,0:T(8,128)}, u32[]{:S(2)}) copy-start(f32[256,512]{1,0:T(8,128)} %get-tuple-element.134) | copy-start | bytes 1572868
Sparse Core Ops, SparseCore 0:
  37.4 33.5 all-reduce.7
  75.0 71.0 all-reduce.5
  202.5 57.4 all-gather.2
  281.7 74.3 all-reduce.9
